TPU v7x, 32 devices: a whole 2x2x4 slice. The times are simulated.
32 devices in a mesh: sample: 4 (over y, x), fsdp: 8 (over z, core).
Axes of the slice: x: 2, y: 2, z: 4, core: 2. Of those that a mesh axis runs over, the one named last changes fastest.
Arguments:
- seed_step: int32 [2], replicated, may hold values from 0 to 16777215
- attn: bfloat16 [16384, 2048], P(('sample', 'fsdp')), may hold values from -6 to 6
- resid: bfloat16 [16384, 4096], P(('sample', 'fsdp')), may hold values from -36 to 36
- cotangent: bfloat16 [16384, 4096], P(('sample', 'fsdp')), may hold values from -6 to 6
- gain: bfloat16 [4096], replicated, may hold values from 0.099609375 to 1.8984375
- mean: float32 [2048, 4096], P('fsdp'), may hold values from -6 to 6
- hess: float32 [2048, 4096], P('fsdp'), may hold values from 0.25 to 4
- momentum: float32 [2048, 4096], P('fsdp'), may hold values from -3 to 3
Outputs:
- new_mean: float32 [2048, 4096], P('fsdp')
- new_hess: float32 [2048, 4096], P('fsdp')
- new_momentum: float32 [2048, 4096], P('fsdp')
All inputs are finite; a program needn't handle non-finite values.
Results may differ from a plain program's by a relative error of at most 0.0035.
Values may be sent and summed in bfloat16 or wider, within the bound.
A program may use at most 192 MiB of HBM per device.

v0:
```python
import jax
import jax.numpy as jnp
from jax import lax
from jax.experimental.layout import Layout, with_layout_constraint
from jax.sharding import PartitionSpec as P

ess_value = 10.0
decay_first = 0.8
decay_second = 0.8
step_size = 0.3
damping = 0.1
norm_eps = 1e-05


def noise_table(seed_step, group_id, row_start, row_count, in_width, width, col_start, col_count):
    row_index = jnp.arange(row_count, dtype=jnp.int32)[:, None] + row_start
    col_index = jnp.arange(col_count, dtype=jnp.int32)[None, :] + col_start
    mixing = (group_id * in_width + row_index) * width + col_index
    mixing = jnp.bitwise_xor(mixing, seed_step[0])
    mixing = mixing * 668265261 + seed_step[1] * 374761393
    mixing = jnp.bitwise_xor(mixing, jnp.right_shift(mixing, 15) & 131071)
    mixing = mixing * 739982445
    mixing = jnp.bitwise_xor(mixing, jnp.right_shift(mixing, 12) & 1048575)
    mixing = mixing * 695872825
    mixing = jnp.bitwise_xor(mixing, jnp.right_shift(mixing, 15) & 131071)
    first_unif = ((mixing & 4095).astype(jnp.float32) + 0.5) / 4096.0
    second_unif = ((jnp.right_shift(mixing, 12) & 4095).astype(jnp.float32) + 0.5) / 4096.0
    return 2.449489742783178 * (first_unif + second_unif - 1.0)


def ivon_update(mean, hess, momentum, grad_sum, curv_sum, groups):
    grad_mean = grad_sum / groups
    hess_est = curv_sum / groups
    new_momentum = decay_first * momentum + (1.0 - decay_first) * grad_mean
    new_hess = (
        decay_second * hess
        + (1.0 - decay_second) * hess_est
        + 0.5 * (1.0 - decay_second) ** 2 * (hess - hess_est) ** 2 / (hess + damping)
    )
    new_mean = mean - step_size * (new_momentum + damping * mean) / (new_hess + damping)
    return (new_mean, new_hess, new_momentum)


def row_major(value):
    return with_layout_constraint(value, Layout(major_to_minor=(0, 1)))


CHUNKS = 4


def per_device(seed_step, attn, resid, cotangent, gain, mean, hess, momentum):
    own_rows = mean.shape[0]
    width = mean.shape[1]
    in_width = attn.shape[1]
    scaling = in_width ** (-0.5)
    groups = lax.axis_size("sample")
    group_id = lax.axis_index("sample")
    shard_id = lax.axis_index("fsdp")
    part = width // CHUNKS
    cuts = [slice(c * part, (c + 1) * part) for c in range(CHUNKS)]
    epsilons, gathered = ([], [])
    for c, cut in enumerate(cuts):
        sigma = 1.0 / jnp.sqrt(ess_value * (hess[:, cut] + damping))
        epsilon = noise_table(
            seed_step, group_id, shard_id * own_rows, own_rows, in_width, width, c * part, part
        )
        sampled = (
            mean[:, cut].astype(jnp.bfloat16).astype(jnp.float32)
            + sigma.astype(jnp.bfloat16).astype(jnp.float32) * epsilon
        ).astype(jnp.bfloat16)
        epsilons.append(epsilon / sigma)
        gathered.append(lax.all_gather(row_major(sampled), "fsdp", axis=0, tiled=True))
    totals = []
    square = jnp.zeros((attn.shape[0], 1), jnp.float32)
    cross = jnp.zeros((attn.shape[0], 1), jnp.float32)
    for c, cut in enumerate(cuts):
        product = row_major(
            jnp.dot(attn, row_major(gathered[c]), preferred_element_type=jnp.float32)
        )
        total = resid[:, cut].astype(jnp.float32) + product * scaling
        upstream = gain[cut].astype(jnp.float32)[None, :] * cotangent[:, cut].astype(jnp.float32)
        square = square + jnp.sum(total * total, axis=-1, keepdims=True)
        cross = cross + jnp.sum(total * upstream, axis=-1, keepdims=True)
        totals.append(total)
    inverse = lax.rsqrt(square / width + norm_eps)
    slope = inverse**3 * (cross / width)
    sums = []
    for c, cut in enumerate(cuts):
        upstream = gain[cut].astype(jnp.float32)[None, :] * cotangent[:, cut].astype(jnp.float32)
        back_low = (inverse * upstream - totals[c] * slope).astype(jnp.bfloat16)
        grad = lax.psum_scatter(
            row_major(
                (
                    lax.dot_general(
                        attn,
                        row_major(back_low),
                        (((0,), (0,)), ((), ())),
                        preferred_element_type=jnp.float32,
                    )
                    * scaling
                ).astype(jnp.bfloat16)
            ),
            "fsdp",
            scatter_dimension=0,
            tiled=True,
        )
        if sums:
            grad, sums[-1] = lax.optimization_barrier((grad, sums[-1]))
        grad = row_major(grad)
        curvature = (grad.astype(jnp.float32) * epsilons[c]).astype(jnp.bfloat16)
        sums.append(lax.psum((grad, row_major(curvature)), "sample"))
    grad_sum = jnp.concatenate([s[0] for s in sums], axis=1).astype(jnp.float32)
    curv_sum = jnp.concatenate([s[1] for s in sums], axis=1).astype(jnp.float32)
    return ivon_update(mean, hess, momentum, grad_sum, curv_sum, groups)


def solution(mesh):
    placed = (
        P(),
        P(("sample", "fsdp"), None),
        P(("sample", "fsdp"), None),
        P(("sample", "fsdp"), None),
        P(),
        P("fsdp", None),
        P("fsdp", None),
        P("fsdp", None),
    )
    return jax.shard_map(
        per_device,
        mesh=mesh,
        in_specs=placed,
        out_specs=(P("fsdp", None), P("fsdp", None), P("fsdp", None)),
        check_vma=False,
    )
```

profile of v0, /device:TPU:0, one launch (start us, length us, event | category | flops | bytes accessed | tf_op | source)
XLA Modules:
  0.0 671.1 jit_solution(17493066383043819291)
XLA Ops:
  13.1 7.5 %add_convert_fusion.1 = (bf16[256,1024]{1,0:T(8,128)(2,1)}, bf16[256,1024]{1,0:T(8,128)(2,1)}, bf16[256,1024]{1,0:T(8,128)(2,1)}, bf16[256,1024]{1,0:T(8,128)(2,1)}) fusion(f32[256,4096]{1,0:T(8,128)} %param.14, bf16[256,4096]{1,0:T(8,128)(2,1)} %convert.6, s32[]{:T(128)} %bitcast.1, s32[]{:T(128)} %bitcast, s32[1024]{0:T(1024)S(1)} %get-tuple-element.54, ...), kind=kLoop, calls=%fused_computation.61 | loop fusion | flops 35651584 | bytes 8401928 | tf_op jit(solution)/shard_map/convert_element_type | solution.py:70
  22.9 47.7 %all-gather.9.cloned.1.call-done = bf16[2048,1024]{1,0:T(8,128)(2,1)} async-done(((bf16[256,1024]{1,0:T(8,128)(2,1)}), bf16[2048,1024]{1,0:T(8,128)(2,1)}) %all-gather.9.cloned.1.call-update) | async-done | bytes 4194320 | tf_op jit(solution)/shard_map/all_gather | solution.py:72
  70.6 6.2 fusion.11
  76.8 41.9 %all-gather.5.cloned.1.call-done = bf16[2048,1024]{1,0:T(8,128)(2,1)} async-done(((bf16[256,1024]{1,0:T(8,128)(2,1)}), bf16[2048,1024]{1,0:T(8,128)(2,1)}) %all-gather.5.cloned.1.call-update) | async-done | bytes 4194320 | tf_op jit(solution)/shard_map/all_gather | solution.py:72
  118.7 6.1 fusion.13
  124.8 41.4 %all-gather.11.cloned.1.call-done = bf16[2048,1024]{1,0:T(8,128)(2,1)} async-done(((bf16[256,1024]{1,0:T(8,128)(2,1)}), bf16[2048,1024]{1,0:T(8,128)(2,1)}) %all-gather.11.cloned.1.call-update) | async-done | bytes 4194320 | tf_op jit(solution)/shard_map/all_gather | solution.py:72
  166.2 6.1 fusion.10
  172.3 41.2 %all-gather.7.cloned.1.call-done = bf16[2048,1024]{1,0:T(8,128)(2,1)} async-done(((bf16[256,1024]{1,0:T(8,128)(2,1)}), bf16[2048,1024]{1,0:T(8,128)(2,1)}) %all-gather.7.cloned.1.call-update) | async-done | bytes 4194320 | tf_op jit(solution)/shard_map/all_gather | solution.py:72
  213.6 9.8 %multiply_reduce_fusion.2 = (f32[512]{0:T(512)S(1)}, f32[512]{0:T(512)S(1)}, f32[512]{0:T(512)S(1)}, f32[512]{0:T(512)S(1)}, f32[512]{0:T(512)S(1)}, /*index=5*/...) fusion(f32[1024]{0:T(1024)S(1)} %get-tuple-element.48, bf16[512,4096]{1,0:T(8,128)(2,1)} %param.11, ...), kind=kOutput, calls=%fused_computation.34 | convolution fusion | flops 2161635328 | bytes 19955712 | tf_op jit(solution)/shard_map/dot_general | solution.py:78
  223.4 5.9 fusion.7
  229.6 6.4 fusion.6
  236.1 42.1 %reduce-scatter.7.cloned.1.call-done = bf16[256,1024]{1,0:T(8,128)(2,1)} async-done(((bf16[2048,1024]{1,0:T(8,128)(2,1)}), bf16[256,1024]{1,0:T(8,128)(2,1)}) %reduce-scatter.7.cloned.1.call-update) | async-done | bytes 524304 | tf_op jit(solution)/shard_map/reduce_scatter | solution.py:91
  278.2 3.9 multiply_convert_fusion.7
  282.2 6.4 fusion.8
  288.7 40.4 %reduce-scatter.5.cloned.1.call-done = bf16[256,1024]{1,0:T(8,128)(2,1)} async-done(((bf16[2048,1024]{1,0:T(8,128)(2,1)}), bf16[256,1024]{1,0:T(8,128)(2,1)}) %reduce-scatter.5.cloned.1.call-update) | async-done | bytes 524304 | tf_op jit(solution)/shard_map/reduce_scatter | solution.py:91
  329.1 53.9 %all-reduce.15.cloned.1.call-done = (bf16[256,1024]{1,0:T(8,128)(2,1)}, bf16[256,1024]{1,0:T(8,128)(2,1)}) async-done(((bf16[256,1024]{1,0:T(8,128)(2,1)}, bf16[256,1024]{1,0:T(8,128)(2,1)}), (bf16[256,1024]{1,0:T(8,128)(2,1)}, bf16[256,1024]{1,0:T(8,128)(2,1)})) %all-reduce.15.cloned.1.call-update) | async-done | bytes 1048592 | tf_op jit(solution)/shard_map/psum | solution.py:111
  383.0 3.9 multiply_convert_fusion.6
  386.9 6.4 fusion.9
  393.5 42.5 %reduce-scatter.9.cloned.1.call-done = bf16[256,1024]{1,0:T(8,128)(2,1)} async-done(((bf16[2048,1024]{1,0:T(8,128)(2,1)}), bf16[256,1024]{1,0:T(8,128)(2,1)}) %reduce-scatter.9.cloned.1.call-update) | async-done | bytes 524304 | tf_op jit(solution)/shard_map/reduce_scatter | solution.py:91
  435.9 53.9 %all-reduce.13.cloned.1.call-done = (bf16[256,1024]{1,0:T(8,128)(2,1)}, bf16[256,1024]{1,0:T(8,128)(2,1)}) async-done(((bf16[256,1024]{1,0:T(8,128)(2,1)}, bf16[256,1024]{1,0:T(8,128)(2,1)}), (bf16[256,1024]{1,0:T(8,128)(2,1)}, bf16[256,1024]{1,0:T(8,128)(2,1)})) %all-reduce.13.cloned.1.call-update) | async-done | bytes 1048592 | tf_op jit(solution)/shard_map/psum | solution.py:111
  494.1 48.6 %reduce-scatter.11.cloned.1.call-done = bf16[256,1024]{1,0:T(8,128)(2,1)} async-done(((bf16[2048,1024]{1,0:T(8,128)(2,1)}), bf16[256,1024]{1,0:T(8,128)(2,1)}) %reduce-scatter.11.cloned.1.call-update) | async-done | bytes 524304 | tf_op jit(solution)/shard_map/reduce_scatter | solution.py:91
  542.6 54.5 %all-reduce.11.cloned.1.call-done = (bf16[256,1024]{1,0:T(8,128)(2,1)}, bf16[256,1024]{1,0:T(8,128)(2,1)}) async-done(((bf16[256,1024]{1,0:T(8,128)(2,1)}, bf16[256,1024]{1,0:T(8,128)(2,1)}), (bf16[256,1024]{1,0:T(8,128)(2,1)}, bf16[256,1024]{1,0:T(8,128)(2,1)})) %all-reduce.11.cloned.1.call-update) | async-done | bytes 1048592 | tf_op jit(solution)/shard_map/psum | solution.py:111
  601.0 52.9 %all-reduce.9.cloned.1.call-done = (bf16[256,1024]{1,0:T(8,128)(2,1)}, bf16[256,1024]{1,0:T(8,128)(2,1)}) async-done(((bf16[256,1024]{1,0:T(8,128)(2,1)}, bf16[256,1024]{1,0:T(8,128)(2,1)}), (bf16[256,1024]{1,0:T(8,128)(2,1)}, bf16[256,1024]{1,0:T(8,128)(2,1)})) %all-reduce.9.cloned.1.call-update) | async-done | bytes 1048592 | tf_op jit(solution)/shard_map/psum | solution.py:111
  653.9 10.4 %divide_subtract_fusion = (f32[256,4096]{1,0:T(8,128)}, f32[256,4096]{1,0:T(8,128)}, f32[256,4096]{1,0:T(8,128)}) fusion(f32[256,4096]{1,0:T(8,128)} %param.13, bf16[256,1024]{1,0:T(8,128)(2,1)} %get-tuple-element.30, bf16[256,1024]{1,0:T(8,128)(2,1)} %get-tuple-element.16, bf16[256,1024]{1,0:T(8,128)(2,1)} %get-tuple-element.14, ...), kind=kLoop, calls=%fused_computation.12 | loop fusion | flops 36700160 | bytes 29360128 | tf_op jit(solution)/shard_map/sub | solution.py:40
  (43 shorter events, 16.1 us)
Async XLA Ops:
  7.2 63.5 %copy-start = (bf16[512,2048]{1,0:T(8,128)(2,1)S(1)}, bf16[512,2048]{1,0:T(8,128)(2,1)}, u32[]{:S(2)}) copy-start(bf16[512,2048]{1,0:T(8,128)(2,1)} %param.9) | copy-start | bytes 6291460
  7.2 63.4 %all-gather.9.cloned.1.call-start = ((), (), s32[]{:S(2)}) async-start(), calls=%async_computation.6 | async-start | bytes 4718592 | tf_op jit(solution)/shard_map/all_gather | solution.py:72
  20.6 2.3 copy-start.3
  20.6 98.1 %all-gather.5.cloned.1.call-start = ((), (), s32[]{:S(2)}) async-start(), calls=%async_computation.4 | async-start | bytes 4718592 | tf_op jit(solution)/shard_map/all_gather | solution.py:72
  21.4 144.8 %all-gather.11.cloned.1.call-start = ((), (), s32[]{:S(2)}) async-start(), calls=%async_computation.7 | async-start | bytes 4718592 | tf_op jit(solution)/shard_map/all_gather | solution.py:72
  22.1 191.4 %all-gather.7.cloned.1.call-start = ((), (), s32[]{:S(2)}) async-start(), calls=%async_computation.5 | async-start | bytes 4718592 | tf_op jit(solution)/shard_map/all_gather | solution.py:72
  22.7 255.5 %reduce-scatter.7.cloned.1.call-start = ((), (), s32[]{:S(2)}) async-start(), calls=%async_computation.9 | async-start | bytes 4718592 | tf_op jit(solution)/shard_map/reduce_scatter | solution.py:91
  213.6 9.8 %copy-start.4 = (f32[512,1024]{1,0:T(8,128)S(1)}, f32[512,1024]{1,0:T(8,128)}, u32[]{:S(2)}) copy-start(f32[512,1024]{1,0:T(8,128)} %fusion.13) | copy-start | bytes 6291460
  229.3 99.8 %reduce-scatter.5.cloned.1.call-start = ((), (), s32[]{:S(2)}) async-start(), calls=%async_computation.8 | async-start | bytes 4718592 | tf_op jit(solution)/shard_map/reduce_scatter | solution.py:91
  236.0 147.0 %all-reduce.15.cloned.1.call-start = ((), (), s32[]{:S(2)}) async-start(), calls=%async_computation.15 | async-start | bytes 2097152 | tf_op jit(solution)/shard_map/psum | solution.py:111
  282.1 153.8 %reduce-scatter.9.cloned.1.call-start = ((), (), s32[]{:S(2)}) async-start(), calls=%async_computation.10 | async-start | bytes 4718592 | tf_op jit(solution)/shard_map/reduce_scatter | solution.py:91
  288.6 201.3 %all-reduce.13.cloned.1.call-start = ((), (), s32[]{:S(2)}) async-start(), calls=%async_computation.14 | async-start | bytes 2097152 | tf_op jit(solution)/shard_map/psum | solution.py:111
  386.9 155.7 %reduce-scatter.11.cloned.1.call-start = ((), (), s32[]{:S(2)}) async-start(), calls=%async_computation.11 | async-start | bytes 4718592 | tf_op jit(solution)/shard_map/reduce_scatter | solution.py:91
  393.4 203.7 %all-reduce.11.cloned.1.call-start = ((), (), s32[]{:S(2)}) async-start(), calls=%async_computation.13 | async-start | bytes 2097152 | tf_op jit(solution)/shard_map/psum | solution.py:111
  493.7 160.2 %copy-start.1 = (bf16[256,1024]{1,0:T(8,128)(2,1)S(1)}, bf16[256,1024]{1,0:T(8,128)(2,1)}, u32[]{:S(2)}) copy-start(bf16[256,1024]{1,0:T(8,128)(2,1)} %get-tuple-element.12) | copy-start | bytes 1572868
  493.7 160.2 %copy-start.2 = (bf16[256,1024]{1,0:T(8,128)(2,1)S(1)}, bf16[256,1024]{1,0:T(8,128)(2,1)}, u32[]{:S(2)}) copy-start(bf16[256,1024]{1,0:T(8,128)(2,1)} %get-tuple-element.18) | copy-start | bytes 1572868
  493.8 160.2 %all-reduce.9.cloned.1.call-start = ((), (), s32[]{:S(2)}) async-start(), calls=%async_computation.12 | async-start | bytes 2097152 | tf_op jit(solution)/shard_map/psum | solution.py:111
Sparse Core Ops, SparseCore 0:
  20.7 49.8 all-gather.8
  72.8 45.8 all-gather.4
  120.3 45.8 all-gather.10
  167.7 45.8 all-gather.6
  229.4 48.7 reduce-scatter.6
  280.9 48.1 reduce-scatter.4
  332.1 50.8 all-reduce.14
  385.9 50.0 reduce-scatter.8
  439.0 50.8 all-reduce.12
  492.6 50.0 reduce-scatter.10
  546.3 50.8 all-reduce.10
  601.1 52.7 all-reduce.8
where the time goes:
time: 672 us; the launch traced here: 671 us
  waiting for transfers between devices  563 us (84%)
  matrix products  53.4 us (8%)
  other arithmetic  37.2 us (6%)
  between operations  14.9 us (2%)
    psum x4, waiting for transfers between devices, per_device(): sums.append(lax.psum((grad, row_major(curvature)), 'sample'))  215 us
    reduce_scatter x4, waiting for transfers between devices, per_device(): lax.psum_scatter(row_major((lax.dot_general(attn, row_major(back_low), ((...  174 us
    all_gather x4, waiting for transfers between devices, per_device(): lax.all_gather(row_major(sampled), 'fsdp', axis=0, tiled=True)  172 us
    dot_general x4, matrix products, per_device(): jnp.dot(attn, row_major(gathered[c]), preferred_element_type=jnp.float32)  28.2 us
    dot_general x4, matrix products, per_device(): lax.dot_general(attn, row_major(back_low), (((0,), (0,)), ((), ())), pref...  25.2 us
    convert_element_type x4, other arithmetic, per_device(): curvature = (grad.astype(jnp.float32) * epsilons[c]).astype(jnp.bfloat16)  15.5 us
  transfers between devices with their start and end apart: 12, of which 12 were waited for; matrix products, arithmetic and copies ran while one was open for 7% of the time, Pallas kernels for 0%

commit v1 on v0

--- a/solution.py
+++ b/solution.py
@@ -10,6 +10,22 @@
 step_size = 0.3
 damping = 0.1
 norm_eps = 1e-05
+
+
+def ring_gather(x, axis, dim):
+    ways, here, step = (lax.axis_size(axis), lax.axis_index(axis), x.shape[dim])
+    shape = [n * ways if d == dim else n for d, n in enumerate(x.shape)]
+    full = lax.dynamic_update_slice_in_dim(jnp.zeros(shape, x.dtype), x, here * step, axis=dim)
+    going_up = going_down = x
+    for far in range(1, ways // 2 + 1):
+        going_up = lax.ppermute(going_up, axis, [(d, (d + 1) % ways) for d in range(ways)])
+        full = lax.dynamic_update_slice_in_dim(full, going_up, (here - far) % ways * step, axis=dim)
+        if 2 * far < ways:
+            going_down = lax.ppermute(going_down, axis, [(d, (d - 1) % ways) for d in range(ways)])
+            full = lax.dynamic_update_slice_in_dim(
+                full, going_down, (here + far) % ways * step, axis=dim
+            )
+    return full
 
 
 def noise_table(seed_step, group_id, row_start, row_count, in_width, width, col_start, col_count):
@@ -69,7 +85,7 @@
             + sigma.astype(jnp.bfloat16).astype(jnp.float32) * epsilon
         ).astype(jnp.bfloat16)
         epsilons.append(epsilon / sigma)
-        gathered.append(lax.all_gather(row_major(sampled), "fsdp", axis=0, tiled=True))
+        gathered.append(ring_gather(row_major(sampled), "fsdp", 0))
     totals = []
     square = jnp.zeros((attn.shape[0], 1), jnp.float32)
     cross = jnp.zeros((attn.shape[0], 1), jnp.float32)

time: 672 us -> 635 us (0.945)
  waiting for transfers between devices: 563 us -> 483 us
  starting transfers between devices: 1.15 us -> 40.2 us
  local copies, waits for them, and re-layouts: 1.41 us -> 19.2 us
  matrix products: 53.4 us -> 35.8 us
    all_gather x4 -> x0, waiting for transfers between devices: 172 us -> none  [per_device(): lax.all_gather(row_major(sampled), 'fsdp', axis=0, tiled=True)]
    ppermute x0 -> x28, waiting for transfers between devices: none -> 93.7 us  [the longest x16 84.3 us: ring_gather(): lax.ppermute(going_up, axis, [(d, (d + 1) % ways) for d in range(ways)])]
    ppermute x0 -> x28, starting transfers between devices: none -> 39.4 us  [the longest x12 28.9 us: ring_gather(): lax.ppermute(going_down, axis, [(d, (d - 1) % ways) for d in range(ways)])]
    dot_general x4, matrix products: 28.2 us -> 11.8 us  [per_device(): jnp.dot(attn, row_major(gathered[c]), preferred_element_type=jnp.float32)]
    dynamic_update_slice x0 -> x28, local copies, waits for them, and re-layouts: none -> 12.8 us  [the longest x16 6.93 us: ring_gather(): lax.dynamic_update_slice_in_dim(full, going_up, (here - far) % ways * ste...]
    dynamic_update_slice x0 -> x4, other arithmetic: none -> 9.9 us  [ring_gather(): lax.dynamic_update_slice_in_dim(jnp.zeros(shape, x.dtype), x, here * step...]
    convert_element_type x1 -> x0, other arithmetic: 7.5 us -> none  [per_device(): sampled = (mean[:, cut].astype(jnp.bfloat16).astype(jnp.float32) + sigma....]
  transfers between devices with their start and end apart: 12 -> 36, of which waited for: 12 -> 28; matrix products, arithmetic and copies ran while one was open for 7% -> 9% of each run, Pallas kernels for 0% -> 0%
where the time goes in v1:
time: 635 us; the launch traced here: 634 us
  waiting for transfers between devices  483 us (76%)
  starting transfers between devices  40.2 us (6%)
  other arithmetic  40 us (6%)
  matrix products  35.8 us (6%)
  local copies, waits for them, and re-layouts  19.2 us (3%)
  between operations  15.4 us (2%)
    psum x4, waiting for transfers between devices, per_device(): sums.append(lax.psum((grad, row_major(curvature)), 'sample'))  215 us
    reduce_scatter x4, waiting for transfers between devices, per_device(): lax.psum_scatter(row_major((lax.dot_general(attn, row_major(back_low), ((...  174 us
    ppermute x16, waiting for transfers between devices, ring_gather(): lax.ppermute(going_up, axis, [(d, (d + 1) % ways) for d in range(ways)])  84.3 us
    ppermute x12, starting transfers between devices, ring_gather(): lax.ppermute(going_down, axis, [(d, (d - 1) % ways) for d in range(ways)])  28.9 us
    dot_general x4, matrix products, per_device(): lax.dot_general(attn, row_major(back_low), (((0,), (0,)), ((), ())), pref...  23.9 us
    convert_element_type x4, other arithmetic, per_device(): curvature = (grad.astype(jnp.float32) * epsilons[c]).astype(jnp.bfloat16)  15.9 us
  transfers between devices with their start and end apart: 36, of which 28 were waited for; matrix products, arithmetic and copies ran while one was open for 9% of the time, Pallas kernels for 0%

profile of v1, /device:TPU:0, one launch (start us, length us, event | category | flops | bytes accessed | tf_op | source)
XLA Modules:
  0.0 634.1 jit_solution(11276024281326858091)
XLA Ops:
  62.5 4.1 collective-permute-done.7
  72.1 5.7 collective-permute-done.16
  77.9 11.2 %collective-permute-done.2 = bf16[256,1024]{1,0:T(8,128)(2,1)S(1)} collective-permute-done((bf16[256,1024]{1,0:T(8,128)(2,1)}, bf16[256,1024]{1,0:T(8,128)(2,1)S(1)}, u32[]{:S(2)}, u32[]{:S(2)}) %collective-permute-start.2) | collective-permute-done | bytes 524320 | tf_op jit(solution)/shard_map/ppermute | solution.py:21
  95.3 5.0 collective-permute-done.23
  106.6 4.9 collective-permute-done.9
  117.0 5.7 collective-permute-done.18
  122.8 11.2 %collective-permute-done.4 = bf16[256,1024]{1,0:T(8,128)(2,1)S(1)} collective-permute-done((bf16[256,1024]{1,0:T(8,128)(2,1)S(1)}, bf16[256,1024]{1,0:T(8,128)(2,1)S(1)}, u32[]{:S(2)}, u32[]{:S(2)}) %collective-permute-start.4) | collective-permute-done | bytes 524320 | tf_op jit(solution)/shard_map/ppermute | solution.py:21
  139.5 5.7 collective-permute-done.25
  145.3 11.2 %collective-permute-done.11 = bf16[256,1024]{1,0:T(8,128)(2,1)S(1)} collective-permute-done((bf16[256,1024]{1,0:T(8,128)(2,1)S(1)}, bf16[256,1024]{1,0:T(8,128)(2,1)S(1)}, u32[]{:S(2)}, u32[]{:S(2)}) %collective-permute-start.11) | collective-permute-done | bytes 524320 | tf_op jit(solution)/shard_map/ppermute | solution.py:21
  159.1 5.7 collective-permute-done.20
  181.7 4.7 multiply_reduce_fusion.2
  186.4 4.6 fusion.7
  191.4 6.4 %fusion.6 = bf16[2048,1024]{1,0:T(8,128)(2,1)} fusion(bf16[512,2048]{1,0:T(8,128)(2,1)S(1)} %copy-done, f32[512,1024]{1,0:T(8,128)} %get-tuple-element.56, f32[512]{0:T(512)S(1)} %get-tuple-element.40, f32[1024]{0:T(1024)S(1)} %get-tuple-element.52, f32[512]{0:T(512)S(1)} %get-tuple-element.41, bf16[512,4096]{1,0:T(8,128)(2,1)} %param.11), kind=kOutput, calls=%fused_computation.14 | convolution fusion | flops 2154823680 | bytes 9445376 | tf_op jit(solution)/shard_map/dot_general | solution.py:110
  197.9 43.3 %reduce-scatter.7.cloned.1.call-done = bf16[256,1024]{1,0:T(8,128)(2,1)} async-done(((bf16[2048,1024]{1,0:T(8,128)(2,1)}), bf16[256,1024]{1,0:T(8,128)(2,1)}) %reduce-scatter.7.cloned.1.call-update) | async-done | bytes 524304 | tf_op jit(solution)/shard_map/reduce_scatter | solution.py:107
  245.3 6.4 %fusion.8 = bf16[2048,1024]{1,0:T(8,128)(2,1)} fusion(bf16[512,2048]{1,0:T(8,128)(2,1)S(1)} %copy-done, f32[512,1024]{1,0:T(8,128)} %copy-done.17, f32[512]{0:T(512)S(1)} %get-tuple-element.40, f32[1024]{0:T(1024)S(1)} %get-tuple-element.50, f32[512]{0:T(512)S(1)} %get-tuple-element.41, bf16[512,4096]{1,0:T(8,128)(2,1)} %param.11), kind=kOutput, calls=%fused_computation.16 | convolution fusion | flops 2154823680 | bytes 9445376 | tf_op jit(solution)/shard_map/dot_general | solution.py:110
  251.8 40.5 %reduce-scatter.5.cloned.1.call-done = bf16[256,1024]{1,0:T(8,128)(2,1)} async-done(((bf16[2048,1024]{1,0:T(8,128)(2,1)}), bf16[256,1024]{1,0:T(8,128)(2,1)}) %reduce-scatter.5.cloned.1.call-update) | async-done | bytes 524304 | tf_op jit(solution)/shard_map/reduce_scatter | solution.py:107
  292.3 53.9 %all-reduce.15.cloned.1.call-done = (bf16[256,1024]{1,0:T(8,128)(2,1)}, bf16[256,1024]{1,0:T(8,128)(2,1)}) async-done(((bf16[256,1024]{1,0:T(8,128)(2,1)}, bf16[256,1024]{1,0:T(8,128)(2,1)}), (bf16[256,1024]{1,0:T(8,128)(2,1)}, bf16[256,1024]{1,0:T(8,128)(2,1)})) %all-reduce.15.cloned.1.call-update) | async-done | bytes 1048592 | tf_op jit(solution)/shard_map/psum | solution.py:127
  350.2 6.4 %fusion.9 = bf16[2048,1024]{1,0:T(8,128)(2,1)} fusion(bf16[512,2048]{1,0:T(8,128)(2,1)S(1)} %copy-done, f32[512,1024]{1,0:T(8,128)} %copy-done.16, f32[512]{0:T(512)S(1)} %get-tuple-element.40, f32[1024]{0:T(1024)S(1)} %get-tuple-element.53, f32[512]{0:T(512)S(1)} %get-tuple-element.41, bf16[512,4096]{1,0:T(8,128)(2,1)} %param.11), kind=kOutput, calls=%fused_computation.17 | convolution fusion | flops 2154823680 | bytes 9445376 | tf_op jit(solution)/shard_map/dot_general | solution.py:110
  356.8 42.2 %reduce-scatter.9.cloned.1.call-done = bf16[256,1024]{1,0:T(8,128)(2,1)} async-done(((bf16[2048,1024]{1,0:T(8,128)(2,1)}), bf16[256,1024]{1,0:T(8,128)(2,1)}) %reduce-scatter.9.cloned.1.call-update) | async-done | bytes 524304 | tf_op jit(solution)/shard_map/reduce_scatter | solution.py:107
  399.0 53.8 %all-reduce.13.cloned.1.call-done = (bf16[256,1024]{1,0:T(8,128)(2,1)}, bf16[256,1024]{1,0:T(8,128)(2,1)}) async-done(((bf16[256,1024]{1,0:T(8,128)(2,1)}, bf16[256,1024]{1,0:T(8,128)(2,1)}), (bf16[256,1024]{1,0:T(8,128)(2,1)}, bf16[256,1024]{1,0:T(8,128)(2,1)})) %all-reduce.13.cloned.1.call-update) | async-done | bytes 1048592 | tf_op jit(solution)/shard_map/psum | solution.py:127
  457.0 48.5 %reduce-scatter.11.cloned.1.call-done = bf16[256,1024]{1,0:T(8,128)(2,1)} async-done(((bf16[2048,1024]{1,0:T(8,128)(2,1)}), bf16[256,1024]{1,0:T(8,128)(2,1)}) %reduce-scatter.11.cloned.1.call-update) | async-done | bytes 524304 | tf_op jit(solution)/shard_map/reduce_scatter | solution.py:107
  505.5 54.5 %all-reduce.11.cloned.1.call-done = (bf16[256,1024]{1,0:T(8,128)(2,1)}, bf16[256,1024]{1,0:T(8,128)(2,1)}) async-done(((bf16[256,1024]{1,0:T(8,128)(2,1)}, bf16[256,1024]{1,0:T(8,128)(2,1)}), (bf16[256,1024]{1,0:T(8,128)(2,1)}, bf16[256,1024]{1,0:T(8,128)(2,1)})) %all-reduce.11.cloned.1.call-update) | async-done | bytes 1048592 | tf_op jit(solution)/shard_map/psum | solution.py:127
  564.0 52.9 %all-reduce.9.cloned.1.call-done = (bf16[256,1024]{1,0:T(8,128)(2,1)}, bf16[256,1024]{1,0:T(8,128)(2,1)}) async-done(((bf16[256,1024]{1,0:T(8,128)(2,1)}, bf16[256,1024]{1,0:T(8,128)(2,1)}), (bf16[256,1024]{1,0:T(8,128)(2,1)}, bf16[256,1024]{1,0:T(8,128)(2,1)})) %all-reduce.9.cloned.1.call-update) | async-done | bytes 1048592 | tf_op jit(solution)/shard_map/psum | solution.py:127
  616.9 10.4 %divide_subtract_fusion = (f32[256,4096]{1,0:T(8,128)}, f32[256,4096]{1,0:T(8,128)}, f32[256,4096]{1,0:T(8,128)}) fusion(f32[256,4096]{1,0:T(8,128)} %param.13, bf16[256,1024]{1,0:T(8,128)(2,1)} %get-tuple-element.30, bf16[256,1024]{1,0:T(8,128)(2,1)} %get-tuple-element.16, bf16[256,1024]{1,0:T(8,128)(2,1)} %get-tuple-element.14, ...), kind=kLoop, calls=%fused_computation.12 | loop fusion | flops 36700160 | bytes 29360128 | tf_op jit(solution)/shard_map/sub | solution.py:56
  (149 shorter events, 119.7 us)
Async XLA Ops:
  7.2 234.0 %reduce-scatter.7.cloned.1.call-start = ((), (), s32[]{:S(2)}) async-start(), calls=%async_computation.5 | async-start | bytes 4718592 | tf_op jit(solution)/shard_map/reduce_scatter | solution.py:107
  18.8 27.3 %collective-permute-start.15 = (bf16[256,1024]{1,0:T(8,128)(2,1)}, bf16[256,1024]{1,0:T(8,128)(2,1)}, u32[]{:S(2)}, u32[]{:S(2)}) collective-permute-start(bf16[256,1024]{1,0:T(8,128)(2,1)} %get-tuple-element.43), channel_id=1, source_target_pairs={{0,7},{1,0},{2,1},{3,2},{4,3},{5,4},{6,5},{7,6},{8,15},{9,8},{10,9... | collective-permute-start | bytes 1572872 | tf_op jit(solution)/shard_map/ppermute | solution.py:24
  26.0 25.5 %collective-permute-start.1 = (bf16[256,1024]{1,0:T(8,128)(2,1)}, bf16[256,1024]{1,0:T(8,128)(2,1)}, u32[]{:S(2)}, u32[]{:S(2)}) collective-permute-start(bf16[256,1024]{1,0:T(8,128)(2,1)} %get-tuple-element.45), channel_id=1, source_target_pairs={{0,7},{1,0},{2,1},{3,2},{4,3},{5,4},{6,5},{7,6},{8,15},{9,8},{10,9... | collective-permute-start | bytes 1572872 | tf_op jit(solution)/shard_map/ppermute | solution.py:24
  51.5 26.3 %collective-permute-start.16 = (bf16[256,1024]{1,0:T(8,128)(2,1)}, bf16[256,1024]{1,0:T(8,128)(2,1)S(1)}, u32[]{:S(2)}, u32[]{:S(2)}) collective-permute-start(bf16[256,1024]{1,0:T(8,128)(2,1)} %collective-permute-done.14), channel_id=1, source_target_pairs={{0,1},{1,2},{2,3},{3,4},{4,5},{5,6},{6,7},{7,0},{8,9},{9,10},{10,1... | collective-permute-start | bytes 1572872 | tf_op jit(solution)/shard_map/ppermute | solution.py:21
  55.5 33.6 %collective-permute-start.2 = (bf16[256,1024]{1,0:T(8,128)(2,1)}, bf16[256,1024]{1,0:T(8,128)(2,1)S(1)}, u32[]{:S(2)}, u32[]{:S(2)}) collective-permute-start(bf16[256,1024]{1,0:T(8,128)(2,1)} %collective-permute-done), channel_id=1, source_target_pairs={{0,1},{1,2},{2,3},{3,4},{4,5},{5,6},{6,7},{7,0},{8,9},{9,10},{10,1... | collective-permute-start | bytes 1572872 | tf_op jit(solution)/shard_map/ppermute | solution.py:21
  57.9 32.0 %collective-permute-start.17 = (bf16[256,1024]{1,0:T(8,128)(2,1)}, bf16[256,1024]{1,0:T(8,128)(2,1)S(1)}, u32[]{:S(2)}, u32[]{:S(2)}) collective-permute-start(bf16[256,1024]{1,0:T(8,128)(2,1)} %collective-permute-done.15), channel_id=1, source_target_pairs={{0,7},{1,0},{2,1},{3,2},{4,3},{5,4},{6,5},{7,6},{8,15},{9,8},{10,9... | collective-permute-start | bytes 1572872 | tf_op jit(solution)/shard_map/ppermute | solution.py:24
  66.6 26.9 %collective-permute-start.3 = (bf16[256,1024]{1,0:T(8,128)(2,1)}, bf16[256,1024]{1,0:T(8,128)(2,1)S(1)}, u32[]{:S(2)}, u32[]{:S(2)}) collective-permute-start(bf16[256,1024]{1,0:T(8,128)(2,1)} %collective-permute-done.1), channel_id=1, source_target_pairs={{0,7},{1,0},{2,1},{3,2},{4,3},{5,4},{6,5},{7,6},{8,15},{9,8},{10,9... | collective-permute-start | bytes 1572872 | tf_op jit(solution)/shard_map/ppermute | solution.py:24
  69.2 31.1 %collective-permute-start.23 = (bf16[256,1024]{1,0:T(8,128)(2,1)}, bf16[256,1024]{1,0:T(8,128)(2,1)S(1)}, u32[]{:S(2)}, u32[]{:S(2)}) collective-permute-start(bf16[256,1024]{1,0:T(8,128)(2,1)} %collective-permute-done.21), channel_id=1, source_target_pairs={{0,1},{1,2},{2,3},{3,4},{4,5},{5,6},{6,7},{7,0},{8,9},{9,10},{10,1... | collective-permute-start | bytes 1572872 | tf_op jit(solution)/shard_map/ppermute | solution.py:21
  93.5 29.3 %collective-permute-start.18 = (bf16[256,1024]{1,0:T(8,128)(2,1)S(1)}, bf16[256,1024]{1,0:T(8,128)(2,1)S(1)}, u32[]{:S(2)}, u32[]{:S(2)}) collective-permute-start(bf16[256,1024]{1,0:T(8,128)(2,1)S(1)} %collective-permute-done.16), channel_id=1, source_target_pairs={{0,1},{1,2},{2,3},{3,4},{4,5},{5,6},{6,7},{7,0},{8,9},{9,10},{10,1... | collective-permute-start | bytes 1572872 | tf_op jit(solution)/shard_map/ppermute | solution.py:21
  100.3 33.7 %collective-permute-start.4 = (bf16[256,1024]{1,0:T(8,128)(2,1)S(1)}, bf16[256,1024]{1,0:T(8,128)(2,1)S(1)}, u32[]{:S(2)}, u32[]{:S(2)}) collective-permute-start(bf16[256,1024]{1,0:T(8,128)(2,1)S(1)} %collective-permute-done.2), channel_id=1, source_target_pairs={{0,1},{1,2},{2,3},{3,4},{4,5},{5,6},{6,7},{7,0},{8,9},{9,10},{10,1... | collective-permute-start | bytes 1572872 | tf_op jit(solution)/shard_map/ppermute | solution.py:21
  102.9 31.2 %collective-permute-start.19 = (bf16[256,1024]{1,0:T(8,128)(2,1)S(1)}, bf16[256,1024]{1,0:T(8,128)(2,1)S(1)}, u32[]{:S(2)}, u32[]{:S(2)}) collective-permute-start(bf16[256,1024]{1,0:T(8,128)(2,1)S(1)} %collective-permute-done.17), channel_id=1, source_target_pairs={{0,7},{1,0},{2,1},{3,2},{4,3},{5,4},{6,5},{7,6},{8,15},{9,8},{10,9... | collective-permute-start | bytes 1572872 | tf_op jit(solution)/shard_map/ppermute | solution.py:24
  111.5 25.8 %collective-permute-start.5 = (bf16[256,1024]{1,0:T(8,128)(2,1)S(1)}, bf16[256,1024]{1,0:T(8,128)(2,1)S(1)}, u32[]{:S(2)}, u32[]{:S(2)}) collective-permute-start(bf16[256,1024]{1,0:T(8,128)(2,1)S(1)} %collective-permute-done.3), channel_id=1, source_target_pairs={{0,7},{1,0},{2,1},{3,2},{4,3},{5,4},{6,5},{7,6},{8,15},{9,8},{10,9... | collective-permute-start | bytes 1572872 | tf_op jit(solution)/shard_map/ppermute | solution.py:24
  114.1 31.1 %collective-permute-start.25 = (bf16[256,1024]{1,0:T(8,128)(2,1)S(1)}, bf16[256,1024]{1,0:T(8,128)(2,1)S(1)}, u32[]{:S(2)}, u32[]{:S(2)}) collective-permute-start(bf16[256,1024]{1,0:T(8,128)(2,1)S(1)} %collective-permute-done.23), channel_id=1, source_target_pairs={{0,1},{1,2},{2,3},{3,4},{4,5},{5,6},{6,7},{7,0},{8,9},{9,10},{10,1... | collective-permute-start | bytes 1572872 | tf_op jit(solution)/shard_map/ppermute | solution.py:21
  122.8 33.7 %collective-permute-start.11 = (bf16[256,1024]{1,0:T(8,128)(2,1)S(1)}, bf16[256,1024]{1,0:T(8,128)(2,1)S(1)}, u32[]{:S(2)}, u32[]{:S(2)}) collective-permute-start(bf16[256,1024]{1,0:T(8,128)(2,1)S(1)} %collective-permute-done.9), channel_id=1, source_target_pairs={{0,1},{1,2},{2,3},{3,4},{4,5},{5,6},{6,7},{7,0},{8,9},{9,10},{10,1... | collective-permute-start | bytes 1572872 | tf_op jit(solution)/shard_map/ppermute | solution.py:21
  137.4 27.4 %collective-permute-start.20 = (bf16[256,1024]{1,0:T(8,128)(2,1)S(1)}, bf16[256,1024]{1,0:T(8,128)(2,1)S(1)}, u32[]{:S(2)}, u32[]{:S(2)}) collective-permute-start(bf16[256,1024]{1,0:T(8,128)(2,1)S(1)} %collective-permute-done.18), channel_id=1, source_target_pairs={{0,1},{1,2},{2,3},{3,4},{4,5},{5,6},{6,7},{7,0},{8,9},{9,10},{10,1... | collective-permute-start | bytes 1572872 | tf_op jit(solution)/shard_map/ppermute | solution.py:21
  145.2 25.1 %collective-permute-start.6 = (bf16[256,1024]{1,0:T(8,128)(2,1)S(1)}, bf16[256,1024]{1,0:T(8,128)(2,1)S(1)}, u32[]{:S(2)}, u32[]{:S(2)}) collective-permute-start(bf16[256,1024]{1,0:T(8,128)(2,1)S(1)} %collective-permute-done.4), channel_id=1, source_target_pairs={{0,1},{1,2},{2,3},{3,4},{4,5},{5,6},{6,7},{7,0},{8,9},{9,10},{10,1... | collective-permute-start | bytes 1572872 | tf_op jit(solution)/shard_map/ppermute | solution.py:21
  156.5 25.1 %collective-permute-start.13 = (bf16[256,1024]{1,0:T(8,128)(2,1)S(1)}, bf16[256,1024]{1,0:T(8,128)(2,1)S(1)}, u32[]{:S(2)}, u32[]{:S(2)}) collective-permute-start(bf16[256,1024]{1,0:T(8,128)(2,1)S(1)} %collective-permute-done.11), channel_id=1, source_target_pairs={{0,1},{1,2},{2,3},{3,4},{4,5},{5,6},{6,7},{7,0},{8,9},{9,10},{10,1... | collective-permute-start | bytes 1572872 | tf_op jit(solution)/shard_map/ppermute | solution.py:21
  191.1 101.2 %reduce-scatter.5.cloned.1.call-start = ((), (), s32[]{:S(2)}) async-start(), calls=%async_computation.4 | async-start | bytes 4718592 | tf_op jit(solution)/shard_map/reduce_scatter | solution.py:107
  197.8 148.4 %all-reduce.15.cloned.1.call-start = ((), (), s32[]{:S(2)}) async-start(), calls=%async_computation.11 | async-start | bytes 2097152 | tf_op jit(solution)/shard_map/psum | solution.py:127
  245.2 153.7 %reduce-scatter.9.cloned.1.call-start = ((), (), s32[]{:S(2)}) async-start(), calls=%async_computation.6 | async-start | bytes 4718592 | tf_op jit(solution)/shard_map/reduce_scatter | solution.py:107
  251.8 201.0 %all-reduce.13.cloned.1.call-start = ((), (), s32[]{:S(2)}) async-start(), calls=%async_computation.10 | async-start | bytes 2097152 | tf_op jit(solution)/shard_map/psum | solution.py:127
  350.2 155.3 %reduce-scatter.11.cloned.1.call-start = ((), (), s32[]{:S(2)}) async-start(), calls=%async_computation.7 | async-start | bytes 4718592 | tf_op jit(solution)/shard_map/reduce_scatter | solution.py:107
  356.7 203.3 %all-reduce.11.cloned.1.call-start = ((), (), s32[]{:S(2)}) async-start(), calls=%async_computation.9 | async-start | bytes 2097152 | tf_op jit(solution)/shard_map/psum | solution.py:127
  456.7 160.2 %all-reduce.9.cloned.1.call-start = ((), (), s32[]{:S(2)}) async-start(), calls=%async_computation.8 | async-start | bytes 2097152 | tf_op jit(solution)/shard_map/psum | solution.py:127
  (30 other events, 1186.5 us)
Sparse Core Ops, SparseCore 0:
  191.2 49.9 reduce-scatter.6
  244.1 48.1 reduce-scatter.4
  295.3 50.8 all-reduce.14
  348.9 49.9 reduce-scatter.8
  401.9 50.8 all-reduce.12
  455.5 50.0 reduce-scatter.10
  509.1 50.8 all-reduce.10
  564.1 52.7 all-reduce.8
